TPU v7x, 1024 devices: a whole 4x4x32 slice. The times are simulated.
1024 devices in a mesh: ctx: 32 (over x, z_hi, core), tp: 32 (over y, z_lo).
Axes of the slice: x: 4, y: 4, z: 32 (z_hi: 4, z_lo: 8; z = z_hi * 8 + z_lo), core: 2. Of those that a mesh axis runs over, the one named last changes fastest.
Arguments:
- query_feats: bfloat16 [8192, 4096], P('tp', 'ctx'), may hold values from -6 to 6
- key_feats: bfloat16 [8192, 4096], P('tp', 'ctx'), may hold values from -6 to 6
- value_feats: bfloat16 [8192, 4096], P('tp', 'ctx'), may hold values from -6 to 6
- out_gate: bfloat16 [8192, 4096], P('tp', 'ctx'), may hold values from -6 to 6
- mr_filter: bfloat16 [512, 128], P('tp'), may hold values from -0.5 to 0.5
- lr_rates: float32 [512, 16], P('tp'), may hold values from 0.00012207031 to 0.1
- lr_residues: float32 [512, 16], P('tp'), may hold values from -6 to 6
- w_out: bfloat16 [8192, 8192], P('tp'), may hold values from -0.125 to 0.125
Outputs:
- mixed_out: bfloat16 [8192, 4096], P('tp', 'ctx')
All inputs are finite; a program needn't handle non-finite values.
Results may differ from a plain program's by a relative error of at most 0.023.
Values may be sent and summed in bfloat16 or wider, within the bound.
No kernel may reach another device: no remote copies, remote signals or barrier semaphores. Data moves between devices by JAX's collectives and lax.ppermute only.
A program may use at most 32 MiB of HBM per device.

v0:
```python
import math

import jax
import jax.numpy as jnp
from jax import lax
from jax.sharding import PartitionSpec as P

chan_group = 16


def passed_along(value, axis, steps):
    count = lax.axis_size(axis)
    first, last = (max(0, -steps), min(count, count - steps))
    return lax.ppermute(value, axis, [(source, source + steps) for source in range(first, last)])


def lr_filter(decay_rates, residues_in, length):
    positions = jnp.arange(length).astype(jnp.float32)
    decays = jnp.exp(-decay_rates[:, :, None] * positions[None, None, :])
    weights = residues_in * jnp.sqrt(2.0 * decay_rates / decay_rates.shape[1])
    return jnp.sum(weights[:, :, None] * decays, axis=1)


def skew(vector, row_count, col_count):
    lead = vector.shape[0]
    full_len = row_count + col_count
    padded = jnp.concatenate([vector, jnp.zeros((lead, 1), vector.dtype)], axis=1)
    rolled = jnp.concatenate([padded[:, row_count - 1 :], padded[:, : row_count - 1]], axis=1)
    tiled = jnp.broadcast_to(rolled[:, None, :], (lead, row_count, full_len)).reshape(
        lead, row_count * full_len
    )
    shaped = tiled[:, : row_count * (full_len - 1)].reshape(lead, row_count, full_len - 1)
    return shaped[:, :, :col_count]


def lag_conv(signal, filter_taps, block_len):
    tap_type = filter_taps.dtype
    group_count, group_chans, length = signal.shape
    tap_count = filter_taps.shape[1]
    block_count = length // block_len
    lag_count = min(block_count, (tap_count + block_len - 2) // block_len + 1)
    blocks = signal.astype(tap_type).reshape(group_count, group_chans, block_count, block_len)
    padded = jnp.concatenate([jnp.zeros_like(blocks), blocks], axis=2)
    extra_len = max(lag_count * block_len - tap_count, 0)
    padded_taps = jnp.concatenate(
        [
            jnp.zeros((group_count, block_len), tap_type),
            filter_taps,
            jnp.zeros((group_count, extra_len), tap_type),
        ],
        axis=1,
    )

    def one_lag(lag_index, running):
        segment = lax.dynamic_slice_in_dim(
            padded_taps, lag_index * block_len + 1, 2 * block_len - 1, 1
        )
        toeplitz = skew(segment, block_len, block_len)
        shifted = lax.dynamic_slice_in_dim(padded, block_count - lag_index, block_count, 2)
        return running + jnp.einsum(
            "gcjs,gst->gcjt",
            shifted,
            toeplitz,
            precision=lax.Precision.HIGHEST,
            preferred_element_type=jnp.float32,
        )

    running = lax.fori_loop(0, lag_count, one_lag, jnp.zeros(blocks.shape, jnp.float32))
    return running.reshape(group_count, group_chans, length)


def medium_tokens(rim_rows, kv_prod, query_feats, mr_filter):
    channels, tokens_here = kv_prod.shape
    rim_len = rim_rows.shape[1]
    local_groups = mr_filter.shape[0]
    extended = jnp.concatenate([rim_rows, kv_prod], axis=1)
    span = tokens_here + rim_len
    padded_taps = jnp.concatenate(
        [
            jnp.zeros((local_groups, span), jnp.bfloat16),
            mr_filter,
            jnp.zeros((local_groups, span), jnp.bfloat16),
        ],
        axis=1,
    )
    vector = padded_taps[:, rim_len + 1 : rim_len + span + tokens_here]
    toeplitz = skew(vector, span, tokens_here)
    medium = jnp.einsum(
        "gcs,gst->gct",
        extended.reshape(local_groups, chan_group, span),
        toeplitz,
        preferred_element_type=jnp.float32,
    )
    return (query_feats.astype(jnp.float32) * medium.reshape(channels, tokens_here)).astype(
        jnp.bfloat16
    )


def per_device(
    query_feats, key_feats, value_feats, out_gate, mr_filter, lr_rates, lr_residues, w_out
):
    channels, tokens_here = key_feats.shape
    ctx_count = lax.axis_size("ctx")
    piece_chans = channels // ctx_count
    length = tokens_here * ctx_count
    block_len = math.gcd(512, length)
    ctx_index = lax.axis_index("ctx")
    group_count = max(piece_chans // chan_group, 1)
    first_group = ctx_index * piece_chans // chan_group
    rim_len = mr_filter.shape[1] - 1
    kv_prod = (key_feats.astype(jnp.float32) * value_feats.astype(jnp.float32)).astype(jnp.bfloat16)
    decay_rates = lax.dynamic_slice_in_dim(lr_rates, first_group, group_count, 0)
    residues_in = lax.dynamic_slice_in_dim(lr_residues, first_group, group_count, 0)
    long_taps = lr_filter(decay_rates, residues_in, length)
    rim_rows = passed_along(kv_prod[:, tokens_here - rim_len :], "ctx", 1)
    gated_mid = medium_tokens(rim_rows, kv_prod, query_feats, mr_filter)
    regrouped = lax.all_to_all(
        gated_mid.reshape(ctx_count, piece_chans, tokens_here),
        "ctx",
        split_axis=0,
        concat_axis=2,
        tiled=True,
    )
    long_out = lag_conv(regrouped, long_taps, block_len).astype(jnp.bfloat16)
    returned = lax.all_to_all(
        long_out.reshape(piece_chans, ctx_count, tokens_here),
        "ctx",
        split_axis=1,
        concat_axis=0,
        tiled=True,
    )
    gated_out = (
        out_gate.astype(jnp.float32) * returned.reshape(channels, tokens_here).astype(jnp.float32)
    ).astype(jnp.bfloat16)
    return lax.psum_scatter(
        lax.dot_general(
            w_out, gated_out, (((0,), (0,)), ((), ())), preferred_element_type=jnp.float32
        ).astype(jnp.bfloat16),
        "tp",
        scatter_dimension=0,
        tiled=True,
    )


def solution(mesh):
    placed = (
        P("tp", "ctx"),
        P("tp", "ctx"),
        P("tp", "ctx"),
        P("tp", "ctx"),
        P("tp", None),
        P("tp", None),
        P("tp", None),
        P("tp", None),
    )
    return jax.shard_map(
        per_device, mesh=mesh, in_specs=placed, out_specs=P("tp", "ctx"), check_vma=False
    )
```

profile of v0, /device:TPU:2, one launch (start us, length us, event | category | flops | bytes accessed | tf_op | source)
XLA Modules:
  0.0 606.8 jit_solution(6720187270477467015)
XLA Ops:
  11.3 4.7 reshape.195
  17.9 9.6 %reshape.196 = bf16[16,255,382]{2,1,0:T(8,128)(2,1)} reshape(bf16[16,97410]{1,0:T(8,128)(2,1)S(1)} %slice-done) | data formatting | bytes 6234240 | tf_op jit(solution)/shard_map/reshape | solution.py:32
  27.5 4.7 collective-permute-done
  34.4 30.7 %all-to-all-start = ((bf16[32,8,128]{2,1,0:T(8,128)(2,1)}), bf16[32,8,128]{2,1,0:T(8,128)(2,1)S(1)}, u32[]{:S(2)}, u32[]{:S(2)}) async-start(bf16[32,8,128]{2,1,0:T(8,128)(2,1)} %bitcast.2), calls=%async_computation | async-start | bytes 131072 | tf_op jit(solution)/shard_map/all_to_all | solution.py:117
  66.3 22.1 %all-to-all-done = bf16[32,8,128]{2,1,0:T(8,128)(2,1)S(1)} async-done(((bf16[32,8,128]{2,1,0:T(8,128)(2,1)}), bf16[32,8,128]{2,1,0:T(8,128)(2,1)S(1)}, u32[]{:S(2)}, u32[]{:S(2)}) %all-to-all-start) | async-done | bytes 65568 | tf_op jit(solution)/shard_map/all_to_all | solution.py:117
  88.5 232.7 %while.16 = (s32[]{:T(128)}, f32[1,8,8,512]{3,2,1,0:T(8,128)S(1)}, f32[1,8,16,512]{3,2,1,0:T(8,128)S(1)}, f32[1,4608]{1,0:T(1,128)S(1)}, s32[]{:T(128)}, /*index...) while((s32[]{:T(128)}, f32[1,8,8,512]{3,2,1,0:T(8,128)S(1)}, ...), condition=%wide.region_2.3_spmd.clone, body=%wide.region_1.2_spmd.clone.sunk | while | flops 201394192 | bytes 16140503 | solution.py:68
  91.2 21.6 %slice_reduce_fusion.2 = f32[523776]{0:T(1024)S(1)} fusion(f32[1,524288]{1,0:T(1,128)S(1)} %bitcast.63), kind=kLoop, calls=%fused_computation.clone.1 | loop fusion | bytes 4190208 | tf_op jit(solution)/shard_map/while/body/eval_jaxpr/slice | solution.py:32
  112.9 2.8 reshape.207
  120.3 21.6 %slice_reduce_fusion.2 = f32[523776]{0:T(1024)S(1)} fusion(f32[1,524288]{1,0:T(1,128)S(1)} %bitcast.63), kind=kLoop, calls=%fused_computation.clone.1 | loop fusion | bytes 4190208 | tf_op jit(solution)/shard_map/while/body/eval_jaxpr/slice | solution.py:32
  141.9 2.8 reshape.207
  149.4 21.6 %slice_reduce_fusion.2 = f32[523776]{0:T(1024)S(1)} fusion(f32[1,524288]{1,0:T(1,128)S(1)} %bitcast.63), kind=kLoop, calls=%fused_computation.clone.1 | loop fusion | bytes 4190208 | tf_op jit(solution)/shard_map/while/body/eval_jaxpr/slice | solution.py:32
  171.0 2.8 reshape.207
  178.5 21.6 %slice_reduce_fusion.2 = f32[523776]{0:T(1024)S(1)} fusion(f32[1,524288]{1,0:T(1,128)S(1)} %bitcast.63), kind=kLoop, calls=%fused_computation.clone.1 | loop fusion | bytes 4190208 | tf_op jit(solution)/shard_map/while/body/eval_jaxpr/slice | solution.py:32
  200.1 2.8 reshape.207
  207.6 21.6 %slice_reduce_fusion.2 = f32[523776]{0:T(1024)S(1)} fusion(f32[1,524288]{1,0:T(1,128)S(1)} %bitcast.63), kind=kLoop, calls=%fused_computation.clone.1 | loop fusion | bytes 4190208 | tf_op jit(solution)/shard_map/while/body/eval_jaxpr/slice | solution.py:32
  229.2 2.8 reshape.207
  236.7 21.6 %slice_reduce_fusion.2 = f32[523776]{0:T(1024)S(1)} fusion(f32[1,524288]{1,0:T(1,128)S(1)} %bitcast.63), kind=kLoop, calls=%fused_computation.clone.1 | loop fusion | bytes 4190208 | tf_op jit(solution)/shard_map/while/body/eval_jaxpr/slice | solution.py:32
  258.3 2.8 reshape.207
  265.8 21.6 %slice_reduce_fusion.2 = f32[523776]{0:T(1024)S(1)} fusion(f32[1,524288]{1,0:T(1,128)S(1)} %bitcast.63), kind=kLoop, calls=%fused_computation.clone.1 | loop fusion | bytes 4190208 | tf_op jit(solution)/shard_map/while/body/eval_jaxpr/slice | solution.py:32
  287.4 2.8 reshape.207
  294.9 21.6 %slice_reduce_fusion.2 = f32[523776]{0:T(1024)S(1)} fusion(f32[1,524288]{1,0:T(1,128)S(1)} %bitcast.63), kind=kLoop, calls=%fused_computation.clone.1 | loop fusion | bytes 4190208 | tf_op jit(solution)/shard_map/while/body/eval_jaxpr/slice | solution.py:32
  321.4 30.8 %all_to_all.8 = bf16[8,32,128]{2,0,1:T(8,128)(2,1)S(1)} all-to-all(bf16[8,32,128]{2,0,1:T(8,128)(2,1)S(1)} %copy.20), channel_id=1, replica_groups=mesh['ctx'=32,'tp'=32] {'ctx'}, dimensions={1} | all-to-all | bytes 131072 | tf_op jit(solution)/shard_map/all_to_all | solution.py:125
  352.2 4.3 fusion.5
  356.5 241.9 %reduce-scatter.2.cloned.1.call-done = bf16[256,128]{0,1:T(8,128)(2,1)} async-done(((bf16[8192,128]{0,1:T(8,128)(2,1)}), bf16[256,128]{0,1:T(8,128)(2,1)}) %reduce-scatter.2.cloned.1.call-update) | async-done | bytes 65552 | tf_op jit(solution)/shard_map/reduce_scatter | solution.py:135
  (80 shorter events, 51.6 us)
Async XLA Ops:
  7.5 24.6 %collective-permute-start = (bf16[256,127]{1,0:T(8,128)(2,1)S(1)}, bf16[256,127]{1,0:T(8,128)(2,1)S(1)}, u32[]{:S(2)}, u32[]{:S(2)}) collective-permute-start(bf16[256,127]{1,0:T(8,128)(2,1)S(1)} %slice.72), channel_id=1, source_target_pairs={{0,32},{32,64},{64,96},{96,128},{128,160},{160,192},{192,224},{224... | collective-permute-start | bytes 195080 | tf_op jit(solution)/shard_map/ppermute | solution.py:14
  16.0 1.9 slice-start
  17.9 15.8 %copy-start.1 = (bf16[256,128]{1,0:T(8,128)(2,1)S(1)}, bf16[256,128]{1,0:T(8,128)(2,1)}, u32[]{:S(2)}) copy-start(bf16[256,128]{1,0:T(8,128)(2,1)} %param.10) | copy-start | bytes 196612
  34.4 54.0 %all-to-all-start = ((bf16[32,8,128]{2,1,0:T(8,128)(2,1)}), bf16[32,8,128]{2,1,0:T(8,128)(2,1)S(1)}, u32[]{:S(2)}, u32[]{:S(2)}) async-start(bf16[32,8,128]{2,1,0:T(8,128)(2,1)} %bitcast.2), calls=%async_computation | async-start | bytes 131072 | tf_op jit(solution)/shard_map/all_to_all | solution.py:117
  65.1 533.3 %reduce-scatter.2.cloned.1.call-start = ((), (), s32[]{:S(2)}) async-start(), calls=%async_computation.3 | async-start | bytes 2162688 | tf_op jit(solution)/shard_map/reduce_scatter | solution.py:135
  88.5 263.7 %copy-start = (bf16[256,128]{1,0:T(8,128)(2,1)S(1)}, bf16[256,128]{1,0:T(8,128)(2,1)}, u32[]{:S(2)}) copy-start(bf16[256,128]{1,0:T(8,128)(2,1)} %param.13) | copy-start | bytes 196612
Sparse Core Ops, SparseCore 0:
  356.6 241.7 reduce-scatter.1
where the time goes:
time: 608 us; the launch traced here: 607 us
  waiting for transfers between devices  269 us (44%)
  local copies, waits for them, and re-layouts  235 us (39%)
  starting transfers between devices  32.9 us (5%)
  blocking collectives  30.8 us (5%)
  matrix products  21.7 us (4%)
  between operations  13.6 us (2%)
    reduce_scatter x1, waiting for transfers between devices, per_device(): lax.psum_scatter(lax.dot_general(w_out, gated_out, (((0,), (0,)), ((), ()...  242 us
    slice x10, local copies, waits for them, and re-layouts, skew(): tiled[:, :row_count * (full_len - 1)].reshape(lead, row_count, full_len - 1)  175 us
    reshape x9, local copies, waits for them, and re-layouts, skew(): tiled[:, :row_count * (full_len - 1)].reshape(lead, row_count, full_len - 1)  31.8 us
    all_to_all x1, blocking collectives, per_device(): lax.all_to_all(long_out.reshape(piece_chans, ctx_count, tokens_here), 'ct...  30.8 us
    all_to_all x1, starting transfers between devices, per_device(): lax.all_to_all(gated_mid.reshape(ctx_count, piece_chans, tokens_here), 'c...  30.7 us
    all_to_all x1, waiting for transfers between devices, per_device(): lax.all_to_all(gated_mid.reshape(ctx_count, piece_chans, tokens_here), 'c...  22.1 us
    while x16, local copies, waits for them, and re-layouts  19.3 us
    dot_general x8, matrix products, one_lag(): jnp.einsum('gcjs,gst->gcjt', shifted, toeplitz, precision=lax.Precision.H...  16 us
  transfers between devices with their start and end apart: 3, of which 3 were waited for; matrix products, arithmetic and copies ran while one was open for 3% of the time, Pallas kernels for 0%

commit v1 on v0

v1 whole, which is shorter than its diff:
```python
import jax
import jax.numpy as jnp
from jax import lax
from jax.experimental import pallas as pl
from jax.experimental.pallas import tpu as pltpu
from jax.sharding import Mesh
from jax.sharding import PartitionSpec as P

chan_group = 16
tp_axes = ("y", "zq", "zb")
f32 = jnp.float32
bf16 = jnp.bfloat16


def split_hi_lo(value):
    hi = value.astype(bf16)
    lo = (value - hi.astype(f32)).astype(bf16)
    return hi, lo


def dot(lhs, rhs):
    return lax.dot_general(lhs, rhs, (((1,), (0,)), ((), ())), preferred_element_type=f32)


def shifted(value, rows):
    pad = jnp.zeros((rows, value.shape[1]), value.dtype)
    return jnp.concatenate([pad, value[: value.shape[0] - rows]], axis=0)


def picked_row(table, row):
    rows = lax.broadcasted_iota(jnp.int32, table.shape, 0)
    return jnp.sum(jnp.where(rows == row, table, 0.0), axis=0, keepdims=True)


def circulant(row, size):
    return pltpu.roll(jnp.broadcast_to(row, (size, size)), 0, 1, stride=1, stride_axis=0)


def filters_kernel(group_ref, feats_ref, taps_ref, rates_ref, residues_ref, out_ref):
    block_count, pair_rows, block = feats_ref.shape
    chans = pair_rows // 2
    rows = block_count * chans
    group = group_ref[0]
    mr_taps = picked_row(taps_ref[...].astype(f32), group)
    rates = picked_row(rates_ref[...], group)
    residues = picked_row(residues_ref[...], group)
    modes = rates.shape[1]

    source = lax.broadcasted_iota(jnp.int32, (block, block), 0)
    target = lax.broadcasted_iota(jnp.int32, (block, block), 1)
    causal = target >= source
    mr_circ = circulant(mr_taps, block)
    mr_toeplitz = jnp.concatenate(
        [jnp.where(causal, mr_circ, 0.0), jnp.where(causal, 0.0, mr_circ)], axis=0
    ).astype(bf16)

    steps = lax.broadcasted_iota(jnp.int32, (block, modes), 0).astype(f32)
    weights = residues * jnp.sqrt(2.0 * rates / modes)
    spread = weights * jnp.exp(-rates * steps)
    collect = jnp.exp(-rates * (block - steps))
    lr_taps = lax.dot_general(
        jnp.ones((8, modes), f32),
        spread,
        (((1,), (1,)), ((), ())),
        precision=lax.Precision.HIGHEST,
        preferred_element_type=f32,
    )[:1]
    lr_hi, lr_lo = split_hi_lo(jnp.where(causal, circulant(lr_taps, block), 0.0))
    collect_hi, collect_lo = split_hi_lo(collect)

    feats = feats_ref[...].astype(f32)
    query = feats[:, :chans].reshape(rows, block)
    kv_prod = feats[:, chans:].reshape(rows, block)
    both = jnp.concatenate([kv_prod, shifted(kv_prod, chans)], axis=1).astype(bf16)
    gated = (query * dot(both, mr_toeplitz)).astype(bf16)

    state = dot(gated, collect_hi) + dot(gated, collect_lo)
    state = shifted(state, chans)
    span = 1
    while span < block_count:
        state = state + jnp.exp(-rates * (block * span)) * shifted(state, chans * span)
        span *= 2
    carried = lax.dot_general(
        state,
        spread,
        (((1,), (1,)), ((), ())),
        precision=lax.Precision.HIGHEST,
        preferred_element_type=f32,
    )
    long_out = dot(gated, lr_hi) + dot(gated, lr_lo) + carried
    out_ref[...] = long_out.reshape(block_count, chans, block).astype(bf16)


def filtered(group, feats, mr_filter, lr_rates, lr_residues):
    block_count, pair_rows, block = feats.shape
    vmem = pl.BlockSpec(memory_space=pltpu.VMEM)
    return pl.pallas_call(
        filters_kernel,
        out_shape=jax.ShapeDtypeStruct((block_count, pair_rows // 2, block), bf16),
        in_specs=[pl.BlockSpec(memory_space=pltpu.SMEM), vmem, vmem, vmem, vmem],
        out_specs=vmem,
    )(group, feats, mr_filter, lr_rates, lr_residues)


def project_kernel(gate_ref, long_ref, w_ref, out_ref, held_ref):
    _, low_count, mid_count, tokens, width = out_ref.shape

    @pl.when(pl.program_id(0) == 0)
    def _():
        product = gate_ref[...].astype(f32) * long_ref[...].astype(f32)
        held_ref[...] = product.T.astype(bf16)

    held = held_ref[...]
    for mid in range(mid_count):
        for low in range(low_count):
            first = (mid * low_count + low) * width
            out_ref[0, low, mid] = dot(held, w_ref[:, first : first + width]).astype(bf16)


def projected(out_gate, long_out, w_out, y_count, mid_count, low_count):
    channels, tokens = out_gate.shape
    width = w_out.shape[1] // (y_count * mid_count * low_count)
    small = pl.BlockSpec((channels, tokens), lambda i: (0, 0))
    return pl.pallas_call(
        project_kernel,
        grid=(y_count,),
        out_shape=jax.ShapeDtypeStruct((y_count, low_count, mid_count, tokens, width), bf16),
        in_specs=[
            small,
            small,
            pl.BlockSpec((channels, mid_count * low_count * width), lambda i: (0, i)),
        ],
        out_specs=pl.BlockSpec(
            (1, low_count, mid_count, tokens, width), lambda i: (i, 0, 0, 0, 0)
        ),
        scratch_shapes=[pltpu.VMEM((tokens, channels), bf16)],
    )(out_gate, long_out, w_out)


def per_device(
    query_feats, key_feats, value_feats, out_gate, mr_filter, lr_rates, lr_residues, w_out
):
    channels, tokens = key_feats.shape
    ctx_count = lax.axis_size("ctx")
    piece = channels // ctx_count
    kv_prod = (key_feats.astype(f32) * value_feats.astype(f32)).astype(bf16)
    pair = jnp.concatenate(
        [query_feats.reshape(ctx_count, piece, tokens), kv_prod.reshape(ctx_count, piece, tokens)],
        axis=1,
    )
    feats = lax.all_to_all(pair, "ctx", split_axis=0, concat_axis=0, tiled=True)
    group = (lax.axis_index("ctx") * piece // chan_group).astype(jnp.int32).reshape(1)
    long_out = filtered(group, feats, mr_filter, lr_rates, lr_residues)
    returned = lax.all_to_all(long_out, "ctx", split_axis=0, concat_axis=0, tiled=True)
    y_count, mid_count, low_count = (lax.axis_size(name) for name in tp_axes)
    partial = projected(
        out_gate, returned.reshape(channels, tokens), w_out, y_count, mid_count, low_count
    )
    width = partial.shape[-1]
    near = lax.all_to_all(
        partial.reshape(y_count * low_count, mid_count, tokens, width),
        ("y", "zb"),
        split_axis=0,
        concat_axis=0,
        tiled=True,
    )
    near_sum = jnp.sum(near.astype(f32), axis=0).astype(bf16)
    far = lax.all_to_all(near_sum, "zq", split_axis=0, concat_axis=0, tiled=True)
    return jnp.sum(far.astype(f32), axis=0).T.astype(bf16)


def solution(mesh):
    ctx_count, tp_count = mesh.devices.shape
    finer = Mesh(
        mesh.devices.reshape(ctx_count, tp_count // 8, 4, 2), ("ctx",) + tp_axes
    )
    tiled = P(tp_axes, "ctx")
    rows = P(tp_axes, None)
    return jax.shard_map(
        per_device,
        mesh=finer,
        in_specs=(tiled, tiled, tiled, tiled, rows, rows, rows, rows),
        out_specs=tiled,
        check_vma=False,
    )
```

time: 608 us -> 162 us (0.27)
  the two profiles are of different devices: /device:TPU:2 before, /device:TPU:1 now
where the time goes in v1:
time: 162 us; the launch traced here: 161 us
  blocking collectives  89.5 us (55%)
  starting transfers between devices  32.4 us (20%)
  waiting for transfers between devices  27.8 us (17%)
  Pallas kernels  7.3 us (5%)
  other arithmetic  2.77 us (2%)
    all_to_all x1, blocking collectives, per_device(): lax.all_to_all(partial.reshape(y_count * low_count, mid_count, tokens, wi...  34.4 us
    all_to_all x1, blocking collectives, per_device(): lax.all_to_all(long_out, 'ctx', split_axis=0, concat_axis=0, tiled=True)  33.2 us
    all_to_all x1, starting transfers between devices, per_device(): feats = lax.all_to_all(pair, 'ctx', split_axis=0, concat_axis=0, tiled=True)  32.4 us
    all_to_all x1, waiting for transfers between devices, per_device(): feats = lax.all_to_all(pair, 'ctx', split_axis=0, concat_axis=0, tiled=True)  27.8 us
    all_to_all x1, blocking collectives, per_device(): lax.all_to_all(near_sum, 'zq', split_axis=0, concat_axis=0, tiled=True)  21.9 us
    pallas_call x1, Pallas kernels, projected(): pl.pallas_call(project_kernel, grid=(y_count,), out_shape=jax.ShapeDtypeS...  4.86 us
  transfers between devices with their start and end apart: 1, of which 1 were waited for; matrix products, arithmetic and copies ran while one was open for 0% of the time, Pallas kernels for 0%

profile of v1, /device:TPU:1, one launch (start us, length us, event | category | flops | bytes accessed | tf_op | source)
XLA Modules:
  0.0 161.2 jit_solution(636434279960148646)
XLA Ops:
  0.0 0.9 fusion
  0.9 1.5 pad_maximum_fusion
  2.4 32.4 %all-to-all-start = ((bf16[32,16,128]{2,1,0:T(8,128)(2,1)}), bf16[32,16,128]{2,1,0:T(8,128)(2,1)S(1)}, u32[]{:S(2)}, u32[]{:S(2)}) async-start(bf16[32,16,128]{2,1,0:T(8,128)(2,1)} %pad_maximum_fusion), calls=%async_computation | async-start | bytes 262144 | tf_op jit(solution)/shard_map/all_to_all | solution.py:151
  34.9 27.8 %all-to-all-done.feats_ref = bf16[32,16,128]{2,1,0:T(8,128)(2,1)S(1)} async-done(((bf16[32,16,128]{2,1,0:T(8,128)(2,1)}), bf16[32,16,128]{2,1,0:T(8,128)(2,1)S(1)}, u32[]{:S(2)}, u32[]{:S(2)}) %all-to-all-start) | async-done | bytes 131104 | tf_op jit(solution)/shard_map/all_to_all | solution.py:151
  62.6 0.0 copy-start
  62.6 0.6 copy-done
  63.3 2.4 %shard_map.82 = bf16[32,8,128]{2,1,0:T(8,128)(2,1)} custom-call(s32[1]{0:T(128)} %bitcast.group_ref, bf16[32,16,128]{2,1,0:T(8,128)(2,1)} %copy-done, bf16[16,128]{1,0:T(8,128)(2,1)} %taps_ref.1, f32[16,16]{1,0:T(8,128)} %rates_ref.1, f32[16,16]{1,0:T(8,128)} %residues_ref.1), custom_call_target="tpu_custom_call" | custom-call | tf_op jit(solution)/shard_map/pallas_call | solution.py:97
  65.7 33.2 %all_to_all.20 = bf16[32,8,128]{2,1,0:T(8,128)(2,1)} all-to-all(bf16[32,8,128]{2,1,0:T(8,128)(2,1)} %shard_map.82), channel_id=1, replica_groups=mesh['ctx'=32,'y'=4,'zq'=4,'zb'=2] {'ctx'}, dimensions={0} | all-to-all | bytes 131072 | tf_op jit(solution)/shard_map/all_to_all | solution.py:154
  98.9 4.9 %shard_map.83 = bf16[4,2,4,128,256]{4,3,2,1,0:T(8,128)(2,1)} custom-call(bf16[256,128]{1,0:T(8,128)(2,1)} %gate_ref.1, bf16[256,128]{1,0:T(8,128)(2,1)} %bitcast.8, bf16[256,8192]{1,0:T(8,128)(2,1)} %w_ref.1), custom_call_target="tpu_custom_call" | custom-call | tf_op jit(solution)/shard_map/pallas_call | solution.py:124
  103.8 34.4 %all_to_all.21 = bf16[8,4,128,256]{3,2,1,0:T(8,128)(2,1)S(1)} all-to-all(bf16[8,4,128,256]{3,2,1,0:T(8,128)(2,1)} %bitcast.7), channel_id=1, replica_groups=mesh['ctx'=32,'y'=4,'zq'=4,'zb'=2] {'y','zb'}, dimensions={0} | all-to-all | bytes 4194304 | tf_op jit(solution)/shard_map/all_to_all | solution.py:160
  138.2 0.3 reduce_sum.24
  138.6 21.9 %all_to_all.22 = bf16[4,128,256]{2,1,0:T(8,128)(2,1)S(1)} all-to-all(bf16[4,128,256]{2,1,0:T(8,128)(2,1)S(1)} %reduce_sum.24), channel_id=1, replica_groups=mesh['ctx'=32,'y'=4,'zq'=4,'zb'=2] {'zq'}, dimensions={0} | all-to-all | bytes 524288 | tf_op jit(solution)/shard_map/all_to_all | solution.py:168
  160.5 0.7 copy.9
  (1 shorter events, 0.0 us)
Async XLA Ops:
  2.4 60.2 %all-to-all-start = ((bf16[32,16,128]{2,1,0:T(8,128)(2,1)}), bf16[32,16,128]{2,1,0:T(8,128)(2,1)S(1)}, u32[]{:S(2)}, u32[]{:S(2)}) async-start(bf16[32,16,128]{2,1,0:T(8,128)(2,1)} %pad_maximum_fusion), calls=%async_computation | async-start | bytes 262144 | tf_op jit(solution)/shard_map/all_to_all | solution.py:151
  62.6 0.6 copy-start

commit v2 on v1

v2 whole, which is shorter than its diff:
```python
import jax
import jax.numpy as jnp
from jax import lax
from jax.experimental import pallas as pl
from jax.experimental.pallas import tpu as pltpu
from jax.sharding import Mesh
from jax.sharding import PartitionSpec as P

chan_group = 16
ctx_axes = ("x", "zh", "co")
tp_axes = ("y", "zq", "zb")
f32 = jnp.float32
bf16 = jnp.bfloat16


def split_hi_lo(value):
    hi = value.astype(bf16)
    lo = (value - hi.astype(f32)).astype(bf16)
    return hi, lo


def dot(lhs, rhs, left=1, right=0, precision=None):
    return lax.dot_general(
        lhs,
        rhs,
        (((left,), (right,)), ((), ())),
        precision=precision,
        preferred_element_type=f32,
    )


def circulant(row, size):
    return pltpu.roll(jnp.broadcast_to(row, (size, size)), 0, 1, stride=1, stride_axis=0)


def same_group(row_count, col_count, row_width):
    rows = lax.broadcasted_iota(jnp.int32, (row_count, col_count), 0) // row_width
    cols = lax.broadcasted_iota(jnp.int32, (row_count, col_count), 1) // chan_group
    return rows == cols


def tables_kernel(taps_ref, rates_ref, residues_ref, mr_ref, lr_ref, collect_ref, spread_ref):
    group_count, block = taps_ref.shape
    mode_rows = rates_ref.shape[0]
    modes = mode_rows // group_count
    source = lax.broadcasted_iota(jnp.int32, (block, block), 0)
    target = lax.broadcasted_iota(jnp.int32, (block, block), 1)
    causal = target >= source

    rates = rates_ref[...]
    steps = lax.broadcasted_iota(jnp.int32, (mode_rows, block), 1).astype(f32)
    spread = residues_ref[...] * jnp.sqrt(2.0 * rates / modes) * jnp.exp(-rates * steps)
    spread_ref[...] = spread
    collect_hi, collect_lo = split_hi_lo(jnp.exp(-rates * (block - steps)))
    collect_ref[0] = collect_hi
    collect_ref[1] = collect_lo
    lr_taps = jnp.sum(spread.reshape(group_count, modes, block), axis=1)
    mr_taps = taps_ref[...].astype(f32)
    for group in range(group_count):
        mr_circ = circulant(mr_taps[group : group + 1], block)
        mr_ref[group, :block] = jnp.where(causal, mr_circ, 0.0).astype(bf16)
        mr_ref[group, block:] = jnp.where(causal, 0.0, mr_circ).astype(bf16)
        lr_circ = jnp.where(causal, circulant(lr_taps[group : group + 1], block), 0.0)
        lr_hi, lr_lo = split_hi_lo(lr_circ)
        lr_ref[group, :, :block] = lr_hi
        lr_ref[group, :, block:] = lr_lo


def blocks_kernel(query_ref, kv_ref, rim_ref, mr_ref, lr_ref, collect_ref, state_ref, local_ref):
    channels, block = kv_ref.shape
    group_count = mr_ref.shape[0]
    modes = state_ref.shape[0]
    both = jnp.concatenate([kv_ref[...], rim_ref[...]], axis=1)
    query = query_ref[...].astype(f32)
    gated_parts = []
    for group in range(group_count):
        rows = slice(group * chan_group, (group + 1) * chan_group)
        medium = dot(both[rows], mr_ref[group])
        gated = (query[rows] * medium).astype(bf16)
        wide = dot(gated, lr_ref[group])
        local_ref[rows] = wide[:, :block] + wide[:, block:]
        gated_parts.append(gated)
    gated = jnp.concatenate(gated_parts, axis=0)
    mixed = dot(collect_ref[0], gated, 1, 1) + dot(collect_ref[1], gated, 1, 1)
    mixed = jnp.where(same_group(group_count * modes, channels, modes), mixed, 0.0)
    state_ref[...] = jnp.sum(mixed.reshape(group_count, modes, channels), axis=0)


def rows_kernel(place_ref, near_ref, rates_ref, out_ref, *, block):
    z_count = out_ref.shape[0]
    near_count = near_ref.shape[0]
    x_here, z_here, core_here = place_ref[0], place_ref[1], place_ref[2]
    span = -block * rates_ref[...]
    for z_to in range(z_count):
        total = jnp.zeros(out_ref.shape[1:], f32)
        target = (x_here * z_count + z_to) * 2 + core_here
        for near in range(near_count):
            source = (near // 2 * z_count + z_here) * 2 + near % 2
            gap = target - 1 - source
            decay = jnp.exp(span * jnp.maximum(gap, 0).astype(f32))
            total = total + jnp.where(gap >= 0, decay, 0.0) * near_ref[near]
        out_ref[z_to] = total


def project_kernel(gate_ref, local_ref, far_ref, spread_ref, w_ref, out_ref, held_ref):
    _, low_count, mid_count, tokens, width = out_ref.shape
    far_count, modes, channels = far_ref.shape

    @pl.when(pl.program_id(0) == 0)
    def _():
        state = far_ref[0]
        for far in range(1, far_count):
            state = state + far_ref[far]
        mode_rows = spread_ref.shape[0]
        wide = jnp.concatenate([state] * (mode_rows // modes), axis=0)
        wide = jnp.where(same_group(mode_rows, channels, modes), wide, 0.0)
        carried = dot(wide, spread_ref[...], 0, 0, lax.Precision.HIGHEST)
        long_out = (local_ref[...] + carried).astype(bf16)
        product = gate_ref[...].astype(f32) * long_out.astype(f32)
        held_ref[...] = product.T.astype(bf16)

    held = held_ref[...]
    for mid in range(mid_count):
        for low in range(low_count):
            first = (mid * low_count + low) * width
            out_ref[0, low, mid] = dot(held, w_ref[:, first : first + width]).astype(bf16)


def per_device(
    query_feats, key_feats, value_feats, out_gate, mr_filter, lr_rates, lr_residues, w_out
):
    channels, tokens = key_feats.shape
    group_count, modes = lr_rates.shape
    ctx_count = lax.axis_size(ctx_axes)
    z_count = lax.axis_size("zh")
    vmem = pl.BlockSpec(memory_space=pltpu.VMEM)
    smem = pl.BlockSpec(memory_space=pltpu.SMEM)

    kv_prod = (key_feats.astype(f32) * value_feats.astype(f32)).astype(bf16)
    rim = lax.ppermute(kv_prod, ctx_axes, [(i, i + 1) for i in range(ctx_count - 1)])
    mode_rows = group_count * modes
    mr_table, lr_table, collect, spread = pl.pallas_call(
        tables_kernel,
        out_shape=(
            jax.ShapeDtypeStruct((group_count, 2 * tokens, tokens), bf16),
            jax.ShapeDtypeStruct((group_count, tokens, 2 * tokens), bf16),
            jax.ShapeDtypeStruct((2, mode_rows, tokens), bf16),
            jax.ShapeDtypeStruct((mode_rows, tokens), f32),
        ),
        in_specs=[vmem] * 3,
        out_specs=(vmem,) * 4,
    )(mr_filter, lr_rates.reshape(mode_rows, 1), lr_residues.reshape(mode_rows, 1))
    rates_wide = jnp.repeat(lr_rates.T, chan_group, axis=1)
    state, local = pl.pallas_call(
        blocks_kernel,
        out_shape=(
            jax.ShapeDtypeStruct((modes, channels), f32),
            jax.ShapeDtypeStruct((channels, tokens), f32),
        ),
        in_specs=[vmem] * 6,
        out_specs=(vmem,) * 2,
    )(query_feats, kv_prod, rim, mr_table, lr_table, collect)
    near_count = lax.axis_size(("x", "co"))
    near_states = lax.all_to_all(
        jnp.broadcast_to(state[None], (near_count, modes, channels)),
        ("x", "co"),
        split_axis=0,
        concat_axis=0,
        tiled=True,
    )
    place = jnp.stack([lax.axis_index(name) for name in ctx_axes]).astype(jnp.int32)
    row_states = pl.pallas_call(
        lambda *refs: rows_kernel(*refs, block=tokens),
        out_shape=jax.ShapeDtypeStruct((z_count, modes, channels), f32),
        in_specs=[smem, vmem, vmem],
        out_specs=vmem,
        name="rows_kernel",
    )(place, near_states, rates_wide)
    far_states = lax.all_to_all(row_states, "zh", split_axis=0, concat_axis=0, tiled=True)

    y_count, mid_count, low_count = (lax.axis_size(name) for name in tp_axes)
    width = w_out.shape[1] // (y_count * mid_count * low_count)
    small = lambda *shape: pl.BlockSpec(shape, lambda i: (0,) * len(shape))
    partial = pl.pallas_call(
        project_kernel,
        grid=(y_count,),
        out_shape=jax.ShapeDtypeStruct((y_count, low_count, mid_count, tokens, width), bf16),
        in_specs=[
            small(channels, tokens),
            small(channels, tokens),
            small(z_count, modes, channels),
            small(mode_rows, tokens),
            pl.BlockSpec((channels, mid_count * low_count * width), lambda i: (0, i)),
        ],
        out_specs=pl.BlockSpec(
            (1, low_count, mid_count, tokens, width), lambda i: (i, 0, 0, 0, 0)
        ),
        scratch_shapes=[pltpu.VMEM((tokens, channels), bf16)],
    )(out_gate, local, far_states, spread, w_out)
    near = lax.all_to_all(
        partial.reshape(y_count * low_count, mid_count, tokens, width),
        ("y", "zb"),
        split_axis=0,
        concat_axis=0,
        tiled=True,
    )
    near_sum = jnp.sum(near.astype(f32), axis=0).astype(bf16)
    far = lax.all_to_all(near_sum, "zq", split_axis=0, concat_axis=0, tiled=True)
    return jnp.sum(far.astype(f32), axis=0).T.astype(bf16)


def solution(mesh):
    ctx_count, tp_count = mesh.devices.shape
    finer = Mesh(
        mesh.devices.reshape(ctx_count // 8, 4, 2, tp_count // 8, 4, 2), ctx_axes + tp_axes
    )
    tiled = P(tp_axes, ctx_axes)
    rows = P(tp_axes, None)
    return jax.shard_map(
        per_device,
        mesh=finer,
        in_specs=(tiled, tiled, tiled, tiled, rows, rows, rows, rows),
        out_specs=tiled,
        check_vma=False,
    )
```

time: 162 us -> 143 us (0.88)
  the two profiles are of different devices: /device:TPU:1 before, /device:TPU:2 now
where the time goes in v2:
time: 143 us; the launch traced here: 142 us
  blocking collectives  93.2 us (65%)
  waiting for transfers between devices  20.1 us (14%)
  Pallas kernels  12.7 us (9%)
  local copies, waits for them, and re-layouts  7.13 us (5%)
  starting transfers between devices  6.78 us (5%)
  other arithmetic  1.9 us (1%)
    all_to_all x1, blocking collectives, per_device(): lax.all_to_all(row_states, 'zh', split_axis=0, concat_axis=0, tiled=True)  43.3 us
    all_to_all x1, blocking collectives, per_device(): lax.all_to_all(partial.reshape(y_count * low_count, mid_count, tokens, wi...  31.2 us
    all_to_all x1, blocking collectives, per_device(): lax.all_to_all(near_sum, 'zq', split_axis=0, concat_axis=0, tiled=True)  18.7 us
    ppermute x1, waiting for transfers between devices, per_device(): lax.ppermute(kv_prod, ctx_axes, [(i, i + 1) for i in range(ctx_count - 1)])  16.9 us
    pallas_call x1, Pallas kernels, per_device(): pl.pallas_call(project_kernel, grid=(y_count,), out_shape=jax.ShapeDtypeS...  5.32 us
    all_to_all x1, starting transfers between devices, per_device(): lax.all_to_all(jnp.broadcast_to(state[None], (near_count, modes, channels...  4.86 us
    all_to_all x1, waiting for transfers between devices, per_device(): lax.all_to_all(jnp.broadcast_to(state[None], (near_count, modes, channels...  3.15 us
    pallas_call x1, Pallas kernels, per_device(): pl.pallas_call(tables_kernel, out_shape=(jax.ShapeDtypeStruct((group_coun...  2.89 us
  transfers between devices with their start and end apart: 2, of which 2 were waited for; matrix products, arithmetic and copies ran while one was open for 3% of the time, Pallas kernels for 2%

profile of v2, /device:TPU:2, one launch (start us, length us, event | category | flops | bytes accessed | tf_op | source)
XLA Modules:
  0.0 141.9 jit_solution(16129529335490654938)
XLA Ops:
  0.0 0.9 multiply_convert_fusion.kv_ref
  0.9 0.0 copy-start.1
  0.9 1.9 %collective-permute-start = (bf16[256,128]{1,0:T(8,128)(2,1)S(1)}, bf16[256,128]{1,0:T(8,128)(2,1)S(1)}, u32[]{:S(2)}, u32[]{:S(2)}) collective-permute-start(bf16[256,128]{1,0:T(8,128)(2,1)S(1)} %multiply_convert_fusion.kv_ref), channel_id=1, source_target_pairs={{0,32},{32,64},{64,96},{96,128},{128,160},{160,192},{192,224},{224... | collective-permute-start | bytes 196616 | tf_op jit(solution)/shard_map/ppermute | solution.py:140
  2.9 1.4 %reshape.18.residues_ref = f32[256,1]{1,0:T(8,128)} reshape(f32[16,16]{1,0:T(8,128)} %param.14) | data formatting | bytes 2048 | tf_op jit(solution)/shard_map/reshape | solution.py:152
  4.3 1.4 %reshape.17.rates_ref = f32[256,1]{1,0:T(8,128)} reshape(f32[16,16]{1,0:T(8,128)} %param.13) | data formatting | bytes 2048 | tf_op jit(solution)/shard_map/reshape | solution.py:152
  5.7 2.9 %shard_map.82 = (bf16[16,256,128]{2,1,0:T(8,128)(2,1)}, bf16[16,128,256]{2,1,0:T(8,128)(2,1)}, bf16[2,256,128]{2,1,0:T(8,128)(2,1)}, f32[256,128]{1,0:T(8,128)}) custom-call(bf16[16,128]{1,0:T(8,128)(2,1)} %taps_ref.1, f32[256,1]{1,0:T(8,128)} %reshape.17.rates_ref, f32[256,1]{1,0:T(8,128)} %reshape.18.residues_ref), custom_call_target="tpu_custom_call" | custom-call | tf_op jit(solution)/shard_map/pallas_call | solution.py:142
  8.6 16.9 %collective-permute-done.rim_ref = bf16[256,128]{1,0:T(8,128)(2,1)S(1)} collective-permute-done((bf16[256,128]{1,0:T(8,128)(2,1)S(1)}, bf16[256,128]{1,0:T(8,128)(2,1)S(1)}, u32[]{:S(2)}, u32[]{:S(2)}) %collective-permute-start) | collective-permute-done | bytes 65568 | tf_op jit(solution)/shard_map/ppermute | solution.py:140
  25.6 0.6 copy-done.2
  26.2 2.8 %shard_map.83 = (f32[16,256]{1,0:T(8,128)}, f32[256,128]{1,0:T(8,128)}) custom-call(bf16[256,128]{1,0:T(8,128)(2,1)} %query_ref.1, bf16[256,128]{1,0:T(8,128)(2,1)} %copy-done.1, bf16[256,128]{1,0:T(8,128)(2,1)} %copy-done.2, bf16[16,256,128]{2,1,0:T(8,128)(2,1)} %get-tuple-element.11.mr_ref, bf16[16,128,256]{2,1,0:T(8,128)(2,1)} %get-tuple-element.12.lr_ref, ...), custom_call_target="tpu_custom_call" | custom-call | tf_op jit(solution)/shard_map/pallas_call | solution.py:154
  29.0 1.4 broadcast_in_dim.4
  30.4 4.9 %all-to-all-start = ((f32[8,16,256]{2,1,0:T(8,128)}), f32[8,16,256]{2,1,0:T(8,128)S(1)}, u32[]{:S(2)}, u32[]{:S(2)}) async-start(f32[8,16,256]{2,1,0:T(8,128)} %broadcast_in_dim.4), calls=%async_computation | async-start | bytes 262144 | tf_op jit(solution)/shard_map/all_to_all | solution.py:164
  35.3 0.1 copy.15
  35.3 0.1 broadcast_in_dim.10
  35.4 0.7 reshape.15.refs_2_
  36.1 0.6 pad_add_fusion.refs_0_
  36.7 3.2 %all-to-all-done.refs_1_ = f32[8,16,256]{2,1,0:T(8,128)S(1)} async-done(((f32[8,16,256]{2,1,0:T(8,128)}), f32[8,16,256]{2,1,0:T(8,128)S(1)}, u32[]{:S(2)}, u32[]{:S(2)}) %all-to-all-start) | async-done | bytes 131104 | tf_op jit(solution)/shard_map/all_to_all | solution.py:164
  39.9 0.6 copy-done
  40.5 1.7 %rows_kernel.1 = f32[4,16,256]{2,1,0:T(8,128)} custom-call(s32[3]{0:T(128)} %pad_add_fusion.refs_0_, f32[8,16,256]{2,1,0:T(8,128)} %copy-done, f32[16,256]{1,0:T(8,128)} %reshape.15.refs_2_), custom_call_target="tpu_custom_call" | custom-call | tf_op jit(solution)/shard_map/rows_kernel/pallas_call | solution.py:172
  42.2 43.3 %all_to_all.20.far_ref = f32[4,16,256]{2,1,0:T(8,128)} all-to-all(f32[4,16,256]{2,1,0:T(8,128)} %rows_kernel.1), channel_id=1, replica_groups=mesh['x'=4,'zh'=4,'co'=2,'y'=4,'zq'=4,'zb'=2] {'zh'}, dimensions={0} | all-to-all | bytes 131072 | tf_op jit(solution)/shard_map/all_to_all | solution.py:179
  85.5 5.3 %shard_map.84 = bf16[4,2,4,128,256]{4,3,2,1,0:T(8,128)(2,1)} custom-call(bf16[256,128]{1,0:T(8,128)(2,1)} %gate_ref.1, f32[256,128]{1,0:T(8,128)} %get-tuple-element.14.local_ref, f32[4,16,256]{2,1,0:T(8,128)} %all_to_all.20.far_ref, f32[256,128]{1,0:T(8,128)} %get-tuple-element.16.spread_ref, bf16[256,8192]{1,0:T(8,128)(2,1)} %w_ref.1), custom_call_target="tpu_custom_call" | custom-call | tf_op jit(solution)/shard_map/pallas_call | solution.py:184
  90.9 31.2 %all_to_all.21 = bf16[8,4,128,256]{3,2,1,0:T(8,128)(2,1)S(1)} all-to-all(bf16[8,4,128,256]{3,2,1,0:T(8,128)(2,1)} %bitcast.6), channel_id=1, replica_groups=mesh['x'=4,'zh'=4,'co'=2,'y'=4,'zq'=4,'zb'=2] {'y','zb'}, dimensions={0} | all-to-all | bytes 4194304 | tf_op jit(solution)/shard_map/all_to_all | solution.py:200
  122.1 0.3 reduce_sum.24
  122.4 18.7 %all_to_all.22 = bf16[4,128,256]{2,1,0:T(8,128)(2,1)S(1)} all-to-all(bf16[4,128,256]{2,1,0:T(8,128)(2,1)S(1)} %reduce_sum.24), channel_id=1, replica_groups=mesh['x'=4,'zh'=4,'co'=2,'y'=4,'zq'=4,'zb'=2] {'zq'}, dimensions={0} | all-to-all | bytes 524288 | tf_op jit(solution)/shard_map/all_to_all | solution.py:208
  141.1 0.7 copy.16
  (6 shorter events, 0.0 us)
Async XLA Ops:
  0.0 35.3 %copy-start.3 = (f32[16,16]{1,0:T(8,128)S(1)}, f32[16,16]{1,0:T(8,128)}, u32[]{:S(2)}) copy-start(f32[16,16]{1,0:T(8,128)} %param.13) | copy-start | bytes 3076
  0.9 24.7 %copy-start.1 = (bf16[256,128]{1,0:T(8,128)(2,1)}, bf16[256,128]{1,0:T(8,128)(2,1)S(1)}, u32[]{:S(2)}) copy-start(bf16[256,128]{1,0:T(8,128)(2,1)S(1)} %multiply_convert_fusion.kv_ref) | copy-start | bytes 196612
  0.9 24.6 %collective-permute-start = (bf16[256,128]{1,0:T(8,128)(2,1)S(1)}, bf16[256,128]{1,0:T(8,128)(2,1)S(1)}, u32[]{:S(2)}, u32[]{:S(2)}) collective-permute-start(bf16[256,128]{1,0:T(8,128)(2,1)S(1)} %multiply_convert_fusion.kv_ref), channel_id=1, source_target_pairs={{0,32},{32,64},{64,96},{96,128},{128,160},{160,192},{192,224},{224... | collective-permute-start | bytes 196616 | tf_op jit(solution)/shard_map/ppermute | solution.py:140
  25.6 0.6 copy-start.2
  30.4 9.5 %all-to-all-start = ((f32[8,16,256]{2,1,0:T(8,128)}), f32[8,16,256]{2,1,0:T(8,128)S(1)}, u32[]{:S(2)}, u32[]{:S(2)}) async-start(f32[8,16,256]{2,1,0:T(8,128)} %broadcast_in_dim.4), calls=%async_computation | async-start | bytes 262144 | tf_op jit(solution)/shard_map/all_to_all | solution.py:164
  39.9 0.6 copy-start

commit v3 on v2

v3 whole, which is shorter than its diff:
```python
import jax
import jax.numpy as jnp
from jax import lax
from jax.experimental import pallas as pl
from jax.experimental.pallas import tpu as pltpu
from jax.sharding import Mesh
from jax.sharding import PartitionSpec as P


chan_group = 16
ctx_axes = ("x", "zh", "co")
tp_axes = ("y", "zq", "zb")
f32 = jnp.float32
bf16 = jnp.bfloat16


def split_hi_lo(value):
    hi = value.astype(bf16)
    lo = (value - hi.astype(f32)).astype(bf16)
    return hi, lo


def dot(lhs, rhs, left=1, right=0, precision=None):
    return lax.dot_general(
        lhs,
        rhs,
        (((left,), (right,)), ((), ())),
        precision=precision,
        preferred_element_type=f32,
    )


def circulant(row, size):
    return pltpu.roll(jnp.broadcast_to(row, (size, size)), 0, 1, stride=1, stride_axis=0)


def same_block(row_count, col_count, row_width, col_width):
    rows = lax.broadcasted_iota(jnp.int32, (row_count, col_count), 0) // row_width
    cols = lax.broadcasted_iota(jnp.int32, (row_count, col_count), 1) // col_width
    return rows == cols


def laid_out(table):
    rows, cols = table.shape
    tiled = jnp.concatenate([table] * rows, axis=1)
    kept = jnp.where(same_block(rows, rows * cols, 1, cols), tiled, 0.0)
    return jnp.sum(kept, axis=0, keepdims=True)


def tables_kernel(
    place_ref,
    taps_ref,
    rates_ref,
    residues_ref,
    gate_ref,
    query_ref,
    mr_ref,
    lr_ref,
    collect_ref,
    spread_ref,
    decay_ref,
    held_gate_ref,
    held_query_ref,
):
    held_gate_ref[...] = gate_ref[...].astype(f32).T
    held_query_ref[...] = query_ref[...].astype(f32)
    group_count, block = taps_ref.shape
    modes = rates_ref.shape[1]
    mode_cols = group_count * modes
    z_count, near_count, _, channels = decay_ref.shape
    source = lax.broadcasted_iota(jnp.int32, (block, block), 0)
    target = lax.broadcasted_iota(jnp.int32, (block, block), 1)
    causal = target >= source

    rates = laid_out(rates_ref[...])
    weights = laid_out(residues_ref[...]) * jnp.sqrt(2.0 * rates / modes)
    steps = lax.broadcasted_iota(jnp.int32, (block, mode_cols), 0).astype(f32)
    spread = weights * jnp.exp(-rates * steps)
    spread_ref[0], spread_ref[1] = split_hi_lo(spread)
    collect = jnp.exp(-rates * (block - steps)).T
    collect_ref[0], collect_ref[1] = split_hi_lo(collect)
    pick = same_block(group_count, mode_cols, 1, modes).astype(f32)
    lr_taps = dot(pick, spread, 1, 1, lax.Precision.HIGHEST)
    mr_taps = taps_ref[...].astype(f32)
    for group in range(group_count):
        mr_circ = circulant(mr_taps[group : group + 1], block)
        mr_ref[group, :block] = jnp.where(causal, mr_circ, 0.0).astype(bf16)
        mr_ref[group, block:] = jnp.where(causal, 0.0, mr_circ).astype(bf16)
        lr_circ = jnp.where(causal, circulant(lr_taps[group : group + 1], block), 0.0)
        lr_hi, lr_lo = split_hi_lo(lr_circ)
        lr_ref[group, :, :block] = lr_hi
        lr_ref[group, :, block:] = lr_lo

    owner = same_block(group_count, channels, 1, chan_group).astype(f32)
    span = -block * dot(rates_ref[...], owner, 0, 0, lax.Precision.HIGHEST)
    x_here, z_here, core_here = place_ref[0], place_ref[1], place_ref[2]
    for z_to in range(z_count):
        into = (x_here * z_count + z_to) * 2 + core_here
        for near in range(near_count):
            out_of = (near // 2 * z_count + z_here) * 2 + near % 2
            gap = into - 1 - out_of
            decay = jnp.exp(span * jnp.maximum(gap, 0).astype(f32))
            decay_ref[z_to, near] = jnp.where(gap >= 0, decay, 0.0)


def blocks_kernel(query_ref, kv_ref, rim_ref, mr_ref, collect_ref, state_ref, gated_ref):
    channels, _ = kv_ref.shape
    group_count = mr_ref.shape[0]
    near_count, modes, _ = state_ref.shape
    both = jnp.concatenate([kv_ref[...], rim_ref[...]], axis=1)
    query = query_ref[...]
    gated_parts = []
    for group in range(group_count):
        rows = slice(group * chan_group, (group + 1) * chan_group)
        medium = dot(both[rows], mr_ref[group])
        gated_parts.append((query[rows] * medium).astype(bf16))
    gated = jnp.concatenate(gated_parts, axis=0)
    gated_ref[...] = gated
    mixed = dot(collect_ref[0], gated, 1, 1) + dot(collect_ref[1], gated, 1, 1)
    mixed = jnp.where(same_block(group_count * modes, channels, modes, chan_group), mixed, 0.0)
    state = jnp.sum(mixed.reshape(group_count, modes, channels), axis=0)
    for near in range(near_count):
        state_ref[near] = state


def local_kernel(gated_ref, lr_ref, local_ref):
    group_count, block, _ = lr_ref.shape
    parts = []
    for group in range(group_count):
        rows = slice(group * chan_group, (group + 1) * chan_group)
        wide = dot(gated_ref[rows], lr_ref[group])
        parts.append(wide[:, :block] + wide[:, block:])
    local_ref[...] = jnp.concatenate(parts, axis=0).T


def rows_kernel(near_ref, decay_ref, out_ref):
    for z_to in range(out_ref.shape[0]):
        total = decay_ref[z_to, 0] * near_ref[0]
        for near in range(1, near_ref.shape[0]):
            total = total + decay_ref[z_to, near] * near_ref[near]
        out_ref[z_to] = total


def project_kernel(gate_ref, local_ref, far_ref, spread_ref, w_hbm, out_ref, w_ref, sems):
    y_count, low_count, mid_count, _, width = out_ref.shape
    span = low_count * mid_count * width
    copies = []
    for y_to in range(y_count):
        cols = slice(y_to * span, (y_to + 1) * span)
        copies.append(
            pltpu.make_async_copy(w_hbm.at[:, cols], w_ref.at[:, cols], sems.at[y_to])
        )
        copies[-1].start()
    far_count, modes, channels = far_ref.shape
    state = far_ref[0]
    for far in range(1, far_count):
        state = state + far_ref[far]
    mode_rows = spread_ref.shape[2]
    wide = jnp.concatenate([state] * (mode_rows // modes), axis=0)
    wide = jnp.where(same_block(mode_rows, channels, modes, chan_group), wide, 0.0)
    wide_hi, wide_lo = split_hi_lo(wide)
    carried = dot(spread_ref[0], wide_hi) + dot(spread_ref[0], wide_lo)
    carried = carried + dot(spread_ref[1], wide_hi)
    long_out = (local_ref[...] + carried).astype(bf16)
    held = (gate_ref[...] * long_out.astype(f32)).astype(bf16)
    for y_to in range(y_count):
        copies[y_to].wait()
        for mid in range(mid_count):
            for low in range(low_count):
                first = ((y_to * mid_count + mid) * low_count + low) * width
                total = dot(held, w_ref[:, first : first + width])
                out_ref[y_to, low, mid] = total.astype(bf16)


def on_chip(kernel, outs, *args, raw=(), scratch=()):
    vmem = pl.BlockSpec(memory_space=pltpu.VMEM)
    smem = pl.BlockSpec(memory_space=pltpu.SMEM)
    specs = [smem if arg.dtype == jnp.int32 else vmem for arg in args]
    placed = [
        arg if arg.dtype == jnp.int32 else pltpu.with_memory_space_constraint(arg, pltpu.VMEM)
        for arg in args
    ]
    specs += [pl.BlockSpec(memory_space=pltpu.HBM)] * len(raw)
    placed += [pltpu.with_memory_space_constraint(arg, pltpu.HBM) for arg in raw]
    return pl.pallas_call(
        kernel,
        out_shape=tuple(pltpu.VMEM(shape, dtype) for shape, dtype in outs),
        in_specs=specs,
        out_specs=(vmem,) * len(outs),
        compiler_params=pltpu.CompilerParams(vmem_limit_bytes=16 << 20),
        scratch_shapes=scratch,
    )(*placed)


def per_device(
    query_feats, key_feats, value_feats, out_gate, mr_filter, lr_rates, lr_residues, w_out
):
    channels, tokens = key_feats.shape
    group_count, modes = lr_rates.shape
    ctx_count = lax.axis_size(ctx_axes)
    z_count = lax.axis_size("zh")
    near_count = lax.axis_size(("x", "co"))
    mode_cols = group_count * modes
    kv_prod = (key_feats.astype(f32) * value_feats.astype(f32)).astype(bf16)
    rim = lax.ppermute(kv_prod, ctx_axes, [(i, i + 1) for i in range(ctx_count - 1)])
    place = jnp.stack([lax.axis_index(name) for name in ctx_axes]).astype(jnp.int32)
    mr_table, lr_table, collect, spread, decays, held_gate, query = on_chip(
        tables_kernel,
        (
            ((group_count, 2 * tokens, tokens), bf16),
            ((group_count, tokens, 2 * tokens), bf16),
            ((2, mode_cols, tokens), bf16),
            ((2, tokens, mode_cols), bf16),
            ((z_count, near_count, modes, channels), f32),
            ((tokens, channels), f32),
            ((channels, tokens), f32),
        ),
        place,
        mr_filter,
        lr_rates,
        lr_residues,
        out_gate,
        query_feats,
    )
    states, gated_mid = on_chip(
        blocks_kernel,
        (((near_count, modes, channels), f32), ((channels, tokens), bf16)),
        query,
        kv_prod,
        rim,
        mr_table,
        collect,
    )
    near_states = lax.all_to_all(
        states, ("x", "co"), split_axis=0, concat_axis=0, tiled=True
    )
    (local,) = on_chip(local_kernel, (((tokens, channels), f32),), gated_mid, lr_table)
    (row_states,) = on_chip(
        rows_kernel, (((z_count, modes, channels), f32),), near_states, decays
    )
    far_states = lax.all_to_all(row_states, "zh", split_axis=0, concat_axis=0, tiled=True)
    y_count, mid_count, low_count = (lax.axis_size(name) for name in tp_axes)
    width = w_out.shape[1] // (y_count * mid_count * low_count)
    (partial,) = on_chip(
        project_kernel,
        (((y_count, low_count, mid_count, tokens, width), bf16),),
        held_gate,
        local,
        far_states,
        spread,
        raw=(w_out,),
        scratch=(pltpu.VMEM(w_out.shape, bf16), pltpu.SemaphoreType.DMA((y_count,))),
    )
    near = lax.all_to_all(
        partial.reshape(y_count * low_count, mid_count, tokens, width),
        ("y", "zb"),
        split_axis=0,
        concat_axis=0,
        tiled=True,
    )
    near_sum = jnp.sum(near.astype(f32), axis=0).astype(bf16)
    far = lax.all_to_all(near_sum, "zq", split_axis=0, concat_axis=0, tiled=True)
    return jnp.sum(far.astype(f32), axis=0).T.astype(bf16)


def solution(mesh):
    ctx_count, tp_count = mesh.devices.shape
    finer = Mesh(
        mesh.devices.reshape(ctx_count // 8, 4, 2, tp_count // 8, 4, 2), ctx_axes + tp_axes
    )
    tiled = P(tp_axes, ctx_axes)
    rows = P(tp_axes, None)
    return jax.shard_map(
        per_device,
        mesh=finer,
        in_specs=(tiled, tiled, tiled, tiled, rows, rows, rows, rows),
        out_specs=tiled,
        check_vma=False,
    )
```

time: 143 us -> 133 us (0.930)
  blocking collectives: 93.2 us -> 59 us
  waiting for transfers between devices: 20.1 us -> 39.7 us
  starting transfers between devices: 6.78 us -> 22.5 us
  Pallas kernels: 12.7 us -> 5.48 us
  local copies, waits for them, and re-layouts: 7.13 us -> 4.49 us
    all_to_all x1, blocking collectives: 43.3 us -> 9.29 us  [per_device(): lax.all_to_all(states, ('x', 'co'), split_axis=0, concat_axis=0, tiled=True)]
    all_to_all x1, waiting for transfers between devices: 3.15 us -> 22.3 us  [per_device(): lax.all_to_all(row_states, 'zh', split_axis=0, concat_axis=0, tiled=True)]
    all_to_all x1, starting transfers between devices: 4.86 us -> 20.6 us  [per_device(): lax.all_to_all(row_states, 'zh', split_axis=0, concat_axis=0, tiled=True)]
    pallas_call x4 -> x5, Pallas kernels: 12.7 us -> 5.48 us  [on_chip(): pl.pallas_call(kernel, out_shape=tuple((pltpu.VMEM(shape, dtype) for shap...]
    reshape x3 -> x0, local copies, waits for them, and re-layouts: 3.59 us -> none  [the longest x1 1.45 us: per_device(): lr_rates.reshape(mode_rows, 1)]
    unnamed x8 -> x10, local copies, waits for them, and re-layouts: 1.27 us -> 3.76 us
    broadcast_in_dim x2 -> x0, local copies, waits for them, and re-layouts: 1.46 us -> none  [the longest x1 1.37 us: per_device(): jnp.broadcast_to(state[None], (near_count, modes, channels))]
  transfers between devices with their start and end apart: 2 -> 2, of which waited for: 2 -> 2; matrix products, arithmetic and copies ran while one was open for 3% -> 0% of each run, Pallas kernels for 2% -> 1%
where the time goes in v3:
time: 133 us
  blocking collectives  59 us (44%)
  waiting for transfers between devices  39.7 us (30%)
  starting transfers between devices  22.5 us (17%)
  Pallas kernels  5.48 us (4%)
  local copies, waits for them, and re-layouts  4.49 us (3%)
  other arithmetic  1.35 us (1%)
    all_to_all x1, blocking collectives, per_device(): lax.all_to_all(partial.reshape(y_count * low_count, mid_count, tokens, wi...  31 us
    all_to_all x1, waiting for transfers between devices, per_device(): lax.all_to_all(row_states, 'zh', split_axis=0, concat_axis=0, tiled=True)  22.3 us
    all_to_all x1, starting transfers between devices, per_device(): lax.all_to_all(row_states, 'zh', split_axis=0, concat_axis=0, tiled=True)  20.6 us
    all_to_all x1, blocking collectives, per_device(): lax.all_to_all(near_sum, 'zq', split_axis=0, concat_axis=0, tiled=True)  18.7 us
    ppermute x1, waiting for transfers between devices, per_device(): lax.ppermute(kv_prod, ctx_axes, [(i, i + 1) for i in range(ctx_count - 1)])  17.4 us
    all_to_all x1, blocking collectives, per_device(): lax.all_to_all(states, ('x', 'co'), split_axis=0, concat_axis=0, tiled=True)  9.29 us
    pallas_call x5, Pallas kernels, on_chip(): pl.pallas_call(kernel, out_shape=tuple((pltpu.VMEM(shape, dtype) for shap...  5.48 us
    unnamed x10, local copies, waits for them, and re-layouts  3.76 us
  transfers between devices with their start and end apart: 2, of which 2 were waited for; matrix products, arithmetic and copies ran while one was open for 0% of the time, Pallas kernels for 1%

profile of v3, /device:TPU:2, one launch (start us, length us, event | category | flops | bytes accessed | tf_op | source)
XLA Modules:
  0.0 132.6 jit_solution(1594090607711061988)
XLA Ops:
  0.0 0.9 multiply_convert_fusion.kv_ref
  0.9 1.9 %collective-permute-start = (bf16[256,128]{1,0:T(8,128)(2,1)S(1)}, bf16[256,128]{1,0:T(8,128)(2,1)S(1)}, u32[]{:S(2)}, u32[]{:S(2)}) collective-permute-start(bf16[256,128]{1,0:T(8,128)(2,1)S(1)} %multiply_convert_fusion.kv_ref), channel_id=1, source_target_pairs={{0,32},{32,64},{64,96},{96,128},{128,160},{160,192},{192,224},{224... | collective-permute-start | bytes 196616 | tf_op jit(solution)/shard_map/ppermute | solution.py:205
  2.8 0.1 pad_add_fusion.place_ref
  2.9 0.0 copy-start
  2.9 0.8 copy-done
  3.7 0.0 copy-start.1
  3.8 0.8 copy-done.1
  4.6 0.0 copy-start.2
  4.6 0.7 copy-done.2
  5.3 0.7 copy-done.3
  6.0 0.7 copy-done.4
  6.7 1.4 %shard_map.82 = (bf16[16,256,128]{2,1,0:T(8,128)(2,1)S(1)}, bf16[16,128,256]{2,1,0:T(8,128)(2,1)S(1)}, bf16[2,256,128]{2,1,0:T(8,128)(2,1)S(1)}, bf16[2,128,256]...) custom-call(s32[3]{0:T(128)S(1)} %pad_add_fusion.place_ref, ...), custom_call_target="tpu_custom_call" | custom-call | tf_op jit(solution)/shard_map/pallas_call | solution.py:185
  8.1 17.4 %collective-permute-done.rim_ref = bf16[256,128]{1,0:T(8,128)(2,1)S(1)} collective-permute-done((bf16[256,128]{1,0:T(8,128)(2,1)S(1)}, bf16[256,128]{1,0:T(8,128)(2,1)S(1)}, u32[]{:S(2)}, u32[]{:S(2)}) %collective-permute-start) | collective-permute-done | bytes 65568 | tf_op jit(solution)/shard_map/ppermute | solution.py:205
  25.5 0.5 shard_map.83
  26.0 9.3 %all_to_all.20.near_ref = f32[8,16,256]{2,1,0:T(8,128)S(1)} all-to-all(f32[8,16,256]{2,1,0:T(8,128)S(1)} %get-tuple-element.20), channel_id=1, replica_groups=mesh['x'=4,'zh'=4,'co'=2,'y'=4,'zq'=4,'zb'=2] {'x','co'}, dimensions={0} | all-to-all | bytes 262144 | tf_op jit(solution)/shard_map/all_to_all | solution.py:234
  35.3 0.7 shard_map.85
  36.0 20.6 %all-to-all-start.1 = ((f32[4,16,256]{2,1,0:T(8,128)}), f32[4,16,256]{2,1,0:T(8,128)S(1)}, u32[]{:S(2)}, u32[]{:S(2)}) async-start(f32[4,16,256]{2,1,0:T(8,128)} %shard_map.85), calls=%async_computation.1 | async-start | bytes 131072 | tf_op jit(solution)/shard_map/all_to_all | solution.py:241
  56.6 0.3 shard_map.84.local_ref
  56.9 22.3 %all-to-all-done.1.far_ref = f32[4,16,256]{2,1,0:T(8,128)S(1)} async-done(((f32[4,16,256]{2,1,0:T(8,128)}), f32[4,16,256]{2,1,0:T(8,128)S(1)}, u32[]{:S(2)}, u32[]{:S(2)}) %all-to-all-start.1) | async-done | bytes 65568 | tf_op jit(solution)/shard_map/all_to_all | solution.py:241
  79.2 2.6 %shard_map.86 = bf16[4,2,4,128,256]{4,3,2,1,0:T(8,128)(2,1)S(1)} custom-call(f32[128,256]{1,0:T(8,128)S(1)} %get-tuple-element.14.gate_ref, f32[128,256]{1,0:T(8,128)S(1)} %shard_map.84.local_ref, f32[4,16,256]{2,1,0:T(8,128)S(1)} %all-to-all-done.1.far_ref, bf16[2,128,256]{2,1,0:T(8,128)(2,1)S(1)} %get-tuple-element.22.spread_ref, bf16[256,8192]{1,0:T(8,128)(2,1)} %w_hbm.1), custom_call_target="tpu_custom_call" | custom-call | tf_op jit(solution)/shard_map/pallas_call | solution.py:185
  81.8 31.0 %all_to_all.21 = bf16[8,4,128,256]{3,2,1,0:T(8,128)(2,1)S(1)} all-to-all(bf16[8,4,128,256]{3,2,1,0:T(8,128)(2,1)S(1)} %bitcast.5), channel_id=1, replica_groups=mesh['x'=4,'zh'=4,'co'=2,'y'=4,'zq'=4,'zb'=2] {'y','zb'}, dimensions={0} | all-to-all | bytes 4194304 | tf_op jit(solution)/shard_map/all_to_all | solution.py:254
  112.8 0.3 reduce_sum.24
  113.2 18.7 %all_to_all.22 = bf16[4,128,256]{2,1,0:T(8,128)(2,1)S(1)} all-to-all(bf16[4,128,256]{2,1,0:T(8,128)(2,1)S(1)} %reduce_sum.24), channel_id=1, replica_groups=mesh['x'=4,'zh'=4,'co'=2,'y'=4,'zq'=4,'zb'=2] {'zq'}, dimensions={0} | all-to-all | bytes 524288 | tf_op jit(solution)/shard_map/all_to_all | solution.py:262
  131.9 0.7 copy.9
  (3 shorter events, 0.0 us)
Async XLA Ops:
  0.9 24.6 %collective-permute-start = (bf16[256,128]{1,0:T(8,128)(2,1)S(1)}, bf16[256,128]{1,0:T(8,128)(2,1)S(1)}, u32[]{:S(2)}, u32[]{:S(2)}) collective-permute-start(bf16[256,128]{1,0:T(8,128)(2,1)S(1)} %multiply_convert_fusion.kv_ref), channel_id=1, source_target_pairs={{0,32},{32,64},{64,96},{96,128},{128,160},{160,192},{192,224},{224... | collective-permute-start | bytes 196616 | tf_op jit(solution)/shard_map/ppermute | solution.py:205
  2.9 0.8 copy-start
  3.7 0.8 copy-start.1
  4.6 0.7 copy-start.2
  5.3 0.7 copy-start.3
  6.0 0.7 copy-start.4
  36.0 43.2 %all-to-all-start.1 = ((f32[4,16,256]{2,1,0:T(8,128)}), f32[4,16,256]{2,1,0:T(8,128)S(1)}, u32[]{:S(2)}, u32[]{:S(2)}) async-start(f32[4,16,256]{2,1,0:T(8,128)} %shard_map.85), calls=%async_computation.1 | async-start | bytes 131072 | tf_op jit(solution)/shard_map/all_to_all | solution.py:241

commit v4 on v3

--- a/solution.py
+++ b/solution.py
@@ -123,14 +123,14 @@
         state_ref[near] = state
 
 
-def local_kernel(gated_ref, lr_ref, local_ref):
+def local_filter(gated_ref, lr_ref):
     group_count, block, _ = lr_ref.shape
     parts = []
     for group in range(group_count):
         rows = slice(group * chan_group, (group + 1) * chan_group)
         wide = dot(gated_ref[rows], lr_ref[group])
         parts.append(wide[:, :block] + wide[:, block:])
-    local_ref[...] = jnp.concatenate(parts, axis=0).T
+    return jnp.concatenate(parts, axis=0).T
 
 
 def rows_kernel(near_ref, decay_ref, out_ref):
@@ -141,7 +141,9 @@
         out_ref[z_to] = total
 
 
-def project_kernel(gate_ref, local_ref, far_ref, spread_ref, w_hbm, out_ref, w_ref, sems):
+def project_kernel(
+    gate_ref, gated_ref, lr_ref, far_ref, spread_ref, w_hbm, out_ref, w_ref, sems
+):
     y_count, low_count, mid_count, _, width = out_ref.shape
     span = low_count * mid_count * width
     copies = []
@@ -161,7 +163,7 @@
     wide_hi, wide_lo = split_hi_lo(wide)
     carried = dot(spread_ref[0], wide_hi) + dot(spread_ref[0], wide_lo)
     carried = carried + dot(spread_ref[1], wide_hi)
-    long_out = (local_ref[...] + carried).astype(bf16)
+    long_out = (local_filter(gated_ref, lr_ref) + carried).astype(bf16)
     held = (gate_ref[...] * long_out.astype(f32)).astype(bf16)
     for y_to in range(y_count):
         copies[y_to].wait()
@@ -234,7 +236,6 @@
     near_states = lax.all_to_all(
         states, ("x", "co"), split_axis=0, concat_axis=0, tiled=True
     )
-    (local,) = on_chip(local_kernel, (((tokens, channels), f32),), gated_mid, lr_table)
     (row_states,) = on_chip(
         rows_kernel, (((z_count, modes, channels), f32),), near_states, decays
     )
@@ -245,7 +246,8 @@
         project_kernel,
         (((y_count, low_count, mid_count, tokens, width), bf16),),
         held_gate,
-        local,
+        gated_mid,
+        lr_table,
         far_states,
         spread,
         raw=(w_out,),

time: 133 us -> 132 us (level)
  blocking collectives: 59 us -> 102 us
  waiting for transfers between devices: 39.7 us -> 17.4 us
  starting transfers between devices: 22.5 us -> 1.92 us
    all_to_all x0 -> x1, blocking collectives: none -> 43 us  [per_device(): lax.all_to_all(row_states, 'zh', split_axis=0, concat_axis=0, tiled=True)]
    all_to_all x1 -> x0, waiting for transfers between devices: 22.3 us -> none  [per_device(): lax.all_to_all(row_states, 'zh', split_axis=0, concat_axis=0, tiled=True)]
    all_to_all x1 -> x0, starting transfers between devices: 20.6 us -> none  [per_device(): lax.all_to_all(row_states, 'zh', split_axis=0, concat_axis=0, tiled=True)]
    pallas_call x5 -> x4, Pallas kernels: 5.48 us -> 4.51 us  [on_chip(): pl.pallas_call(kernel, out_shape=tuple((pltpu.VMEM(shape, dtype) for shap...]
  transfers between devices with their start and end apart: 2 -> 1, of which waited for: 2 -> 1; matrix products, arithmetic and copies ran while one was open for 0% -> 0% of each run, Pallas kernels for 1% -> 1%
where the time goes in v4:
time: 132 us
  blocking collectives  102 us (77%)
  waiting for transfers between devices  17.4 us (13%)
  Pallas kernels  4.51 us (3%)
  local copies, waits for them, and re-layouts  4.49 us (3%)
  starting transfers between devices  1.92 us (1%)
  other arithmetic  1.35 us (1%)
    all_to_all x1, blocking collectives, per_device(): lax.all_to_all(row_states, 'zh', split_axis=0, concat_axis=0, tiled=True)  43 us
    all_to_all x1, blocking collectives, per_device(): lax.all_to_all(partial.reshape(y_count * low_count, mid_count, tokens, wi...  31 us
    all_to_all x1, blocking collectives, per_device(): lax.all_to_all(near_sum, 'zq', split_axis=0, concat_axis=0, tiled=True)  18.7 us
    ppermute x1, waiting for transfers between devices, per_device(): lax.ppermute(kv_prod, ctx_axes, [(i, i + 1) for i in range(ctx_count - 1)])  17.4 us
    all_to_all x1, blocking collectives, per_device(): lax.all_to_all(states, ('x', 'co'), split_axis=0, concat_axis=0, tiled=True)  9.29 us
    pallas_call x4, Pallas kernels, on_chip(): pl.pallas_call(kernel, out_shape=tuple((pltpu.VMEM(shape, dtype) for shap...  4.51 us
    unnamed x10, local copies, waits for them, and re-layouts  3.76 us
  transfers between devices with their start and end apart: 1, of which 1 were waited for; matrix products, arithmetic and copies ran while one was open for 0% of the time, Pallas kernels for 1%

profile of v4, /device:TPU:2, one launch (start us, length us, event | category | flops | bytes accessed | tf_op | source)
XLA Modules:
  0.0 131.8 jit_solution(15545438955022128559)
XLA Ops:
  0.0 0.9 multiply_convert_fusion.kv_ref
  0.9 1.9 %collective-permute-start = (bf16[256,128]{1,0:T(8,128)(2,1)S(1)}, bf16[256,128]{1,0:T(8,128)(2,1)S(1)}, u32[]{:S(2)}, u32[]{:S(2)}) collective-permute-start(bf16[256,128]{1,0:T(8,128)(2,1)S(1)} %multiply_convert_fusion.kv_ref), channel_id=1, source_target_pairs={{0,32},{32,64},{64,96},{96,128},{128,160},{160,192},{192,224},{224... | collective-permute-start | bytes 196616 | tf_op jit(solution)/shard_map/ppermute | solution.py:207
  2.8 0.1 pad_add_fusion.place_ref
  2.9 0.0 copy-start
  2.9 0.8 copy-done
  3.7 0.0 copy-start.1
  3.8 0.8 copy-done.1
  4.6 0.0 copy-start.2
  4.6 0.7 copy-done.2
  5.3 0.0 copy-start.3
  5.3 0.7 copy-done.3
  6.0 0.0 copy-start.4
  6.0 0.7 copy-done.4
  6.7 1.4 %shard_map.82 = (bf16[16,256,128]{2,1,0:T(8,128)(2,1)S(1)}, bf16[16,128,256]{2,1,0:T(8,128)(2,1)S(1)}, bf16[2,256,128]{2,1,0:T(8,128)(2,1)S(1)}, bf16[2,128,256]...) custom-call(s32[3]{0:T(128)S(1)} %pad_add_fusion.place_ref, ...), custom_call_target="tpu_custom_call" | custom-call | tf_op jit(solution)/shard_map/pallas_call | solution.py:187
  8.1 17.4 %collective-permute-done.rim_ref = bf16[256,128]{1,0:T(8,128)(2,1)S(1)} collective-permute-done((bf16[256,128]{1,0:T(8,128)(2,1)S(1)}, bf16[256,128]{1,0:T(8,128)(2,1)S(1)}, u32[]{:S(2)}, u32[]{:S(2)}) %collective-permute-start) | collective-permute-done | bytes 65568 | tf_op jit(solution)/shard_map/ppermute | solution.py:207
  25.5 0.5 shard_map.83
  26.0 9.3 %all_to_all.20.near_ref = f32[8,16,256]{2,1,0:T(8,128)S(1)} all-to-all(f32[8,16,256]{2,1,0:T(8,128)S(1)} %get-tuple-element.20), channel_id=1, replica_groups=mesh['x'=4,'zh'=4,'co'=2,'y'=4,'zq'=4,'zb'=2] {'x','co'}, dimensions={0} | all-to-all | bytes 262144 | tf_op jit(solution)/shard_map/all_to_all | solution.py:236
  35.4 43.0 %all_to_all.21.far_ref = f32[4,16,256]{2,1,0:T(8,128)S(1)} all-to-all(f32[4,16,256]{2,1,0:T(8,128)S(1)} %shard_map.84), channel_id=1, replica_groups=mesh['x'=4,'zh'=4,'co'=2,'y'=4,'zq'=4,'zb'=2] {'zh'}, dimensions={0} | all-to-all | bytes 131072 | tf_op jit(solution)/shard_map/all_to_all | solution.py:242
  78.4 2.5 %shard_map.85 = bf16[4,2,4,128,256]{4,3,2,1,0:T(8,128)(2,1)S(1)} custom-call(f32[128,256]{1,0:T(8,128)S(1)} %get-tuple-element.14.gate_ref, bf16[256,128]{1,0:T(8,128)(2,1)S(1)} %get-tuple-element.18.gated_ref, bf16[16,128,256]{2,1,0:T(8,128)(2,1)S(1)} %get-tuple-element.19.lr_ref, f32[4,16,256]{2,1,0:T(8,128)S(1)} %all_to_all.21.far_ref, ...), custom_call_target="tpu_custom_call" | custom-call | tf_op jit(solution)/shard_map/pallas_call | solution.py:187
  80.9 31.0 %all_to_all.22 = bf16[8,4,128,256]{3,2,1,0:T(8,128)(2,1)S(1)} all-to-all(bf16[8,4,128,256]{3,2,1,0:T(8,128)(2,1)S(1)} %bitcast.5), channel_id=1, replica_groups=mesh['x'=4,'zh'=4,'co'=2,'y'=4,'zq'=4,'zb'=2] {'y','zb'}, dimensions={0} | all-to-all | bytes 4194304 | tf_op jit(solution)/shard_map/all_to_all | solution.py:256
  112.0 0.3 reduce_sum.24
  112.3 18.7 %all_to_all.23 = bf16[4,128,256]{2,1,0:T(8,128)(2,1)S(1)} all-to-all(bf16[4,128,256]{2,1,0:T(8,128)(2,1)S(1)} %reduce_sum.24), channel_id=1, replica_groups=mesh['x'=4,'zh'=4,'co'=2,'y'=4,'zq'=4,'zb'=2] {'zq'}, dimensions={0} | all-to-all | bytes 524288 | tf_op jit(solution)/shard_map/all_to_all | solution.py:264
  131.0 0.7 copy.9
  (2 shorter events, 0.1 us)
Async XLA Ops:
  0.9 24.6 %collective-permute-start = (bf16[256,128]{1,0:T(8,128)(2,1)S(1)}, bf16[256,128]{1,0:T(8,128)(2,1)S(1)}, u32[]{:S(2)}, u32[]{:S(2)}) collective-permute-start(bf16[256,128]{1,0:T(8,128)(2,1)S(1)} %multiply_convert_fusion.kv_ref), channel_id=1, source_target_pairs={{0,32},{32,64},{64,96},{96,128},{128,160},{160,192},{192,224},{224... | collective-permute-start | bytes 196616 | tf_op jit(solution)/shard_map/ppermute | solution.py:207
  2.9 0.8 copy-start
  3.7 0.8 copy-start.1
  4.6 0.7 copy-start.2
  5.3 0.7 copy-start.3
  6.0 0.7 copy-start.4

commit v5 on v4

--- a/solution.py
+++ b/solution.py
@@ -144,7 +144,7 @@
 def project_kernel(
     gate_ref, gated_ref, lr_ref, far_ref, spread_ref, w_hbm, out_ref, w_ref, sems
 ):
-    y_count, low_count, mid_count, _, width = out_ref.shape
+    low_count, y_count, mid_count, _, width = out_ref.shape
     span = low_count * mid_count * width
     copies = []
     for y_to in range(y_count):
@@ -171,7 +171,14 @@
             for low in range(low_count):
                 first = ((y_to * mid_count + mid) * low_count + low) * width
                 total = dot(held, w_ref[:, first : first + width])
-                out_ref[y_to, low, mid] = total.astype(bf16)
+                out_ref[low, y_to, mid] = total.astype(bf16)
+
+
+def mixed_kernel(far_ref, out_ref):
+    total = far_ref[0].astype(f32)
+    for far in range(1, far_ref.shape[0]):
+        total = total + far_ref[far].astype(f32)
+    out_ref[...] = total.T.astype(bf16)
 
 
 def on_chip(kernel, outs, *args, raw=(), scratch=()):
@@ -244,7 +251,7 @@
     width = w_out.shape[1] // (y_count * mid_count * low_count)
     (partial,) = on_chip(
         project_kernel,
-        (((y_count, low_count, mid_count, tokens, width), bf16),),
+        (((low_count, y_count, mid_count, tokens, width), bf16),),
         held_gate,
         gated_mid,
         lr_table,
@@ -255,14 +262,20 @@
     )
     near = lax.all_to_all(
         partial.reshape(y_count * low_count, mid_count, tokens, width),
-        ("y", "zb"),
+        ("zb", "y"),
         split_axis=0,
         concat_axis=0,
         tiled=True,
     )
     near_sum = jnp.sum(near.astype(f32), axis=0).astype(bf16)
     far = lax.all_to_all(near_sum, "zq", split_axis=0, concat_axis=0, tiled=True)
-    return jnp.sum(far.astype(f32), axis=0).T.astype(bf16)
+    return pl.pallas_call(
+        mixed_kernel,
+        out_shape=jax.ShapeDtypeStruct((width, tokens), bf16),
+        in_specs=[pl.BlockSpec(memory_space=pltpu.VMEM)],
+        out_specs=pl.BlockSpec(memory_space=pltpu.VMEM),
+        compiler_params=pltpu.CompilerParams(vmem_limit_bytes=16 << 20),
+    )(pltpu.with_memory_space_constraint(far, pltpu.VMEM))
 
 
 def solution(mesh):

time: 132 us -> 132 us (level)
  the two profiles are of different devices: /device:TPU:2 before, /device:TPU:8 now
where the time goes in v5:
time: 132 us
  blocking collectives  119 us (90%)
  Pallas kernels  5.25 us (4%)
  local copies, waits for them, and re-layouts  3.76 us (3%)
  starting transfers between devices  1.74 us (1%)
    all_to_all x1, blocking collectives, per_device(): lax.all_to_all(row_states, 'zh', split_axis=0, concat_axis=0, tiled=True)  43 us
    all_to_all x1, blocking collectives, per_device(): lax.all_to_all(partial.reshape(y_count * low_count, mid_count, tokens, wi...  29.6 us
    all_to_all x1, blocking collectives, per_device(): lax.all_to_all(states, ('x', 'co'), split_axis=0, concat_axis=0, tiled=True)  27.8 us
    all_to_all x1, blocking collectives, per_device(): lax.all_to_all(near_sum, 'zq', split_axis=0, concat_axis=0, tiled=True)  19 us
    pallas_call x4, Pallas kernels, on_chip(): pl.pallas_call(kernel, out_shape=tuple((pltpu.VMEM(shape, dtype) for shap...  4.51 us
    unnamed x10, local copies, waits for them, and re-layouts  3.76 us
  transfers between devices with their start and end apart: 1, of which 0 were waited for; matrix products, arithmetic and copies ran while one was open for 0% of the time, Pallas kernels for 1%

profile of v5, /device:TPU:8, one launch (start us, length us, event | category | flops | bytes accessed | tf_op | source)
XLA Modules:
  0.0 131.5 jit_solution(12647267844630154381)
XLA Ops:
  0.0 0.9 multiply_convert_fusion.kv_ref
  0.9 1.7 %collective-permute-start = (bf16[256,128]{1,0:T(8,128)(2,1)S(1)}, bf16[256,128]{1,0:T(8,128)(2,1)S(1)}, u32[]{:S(2)}, u32[]{:S(2)}) collective-permute-start(bf16[256,128]{1,0:T(8,128)(2,1)S(1)} %multiply_convert_fusion.kv_ref), channel_id=1, source_target_pairs={{0,32},{32,64},{64,96},{96,128},{128,160},{160,192},{192,224},{224... | collective-permute-start | bytes 196616 | tf_op jit(solution)/shard_map/ppermute | solution.py:214
  2.7 0.1 pad_add_fusion.place_ref
  2.7 0.0 copy-start
  2.7 0.8 copy-done
  3.6 0.0 copy-start.1
  3.6 0.8 copy-done.1
  4.4 0.0 copy-start.2
  4.4 0.7 copy-done.2
  5.1 0.0 copy-start.3
  5.1 0.7 copy-done.3
  5.8 0.0 copy-start.4
  5.8 0.7 copy-done.4
  6.5 1.4 %shard_map.82 = (bf16[16,256,128]{2,1,0:T(8,128)(2,1)S(1)}, bf16[16,128,256]{2,1,0:T(8,128)(2,1)S(1)}, bf16[2,256,128]{2,1,0:T(8,128)(2,1)S(1)}, bf16[2,128,256]...) custom-call(s32[3]{0:T(128)S(1)} %pad_add_fusion.place_ref, ...), custom_call_target="tpu_custom_call" | custom-call | tf_op jit(solution)/shard_map/pallas_call | solution.py:194
  7.9 0.0 collective-permute-done.rim_ref
  8.0 0.5 shard_map.83
  8.4 27.8 %all_to_all.20.near_ref = f32[8,16,256]{2,1,0:T(8,128)S(1)} all-to-all(f32[8,16,256]{2,1,0:T(8,128)S(1)} %get-tuple-element.20), channel_id=1, replica_groups=mesh['x'=4,'zh'=4,'co'=2,'y'=4,'zq'=4,'zb'=2] {'x','co'}, dimensions={0} | all-to-all | bytes 262144 | tf_op jit(solution)/shard_map/all_to_all | solution.py:243
  36.3 43.0 %all_to_all.21.far_ref = f32[4,16,256]{2,1,0:T(8,128)S(1)} all-to-all(f32[4,16,256]{2,1,0:T(8,128)S(1)} %shard_map.84), channel_id=1, replica_groups=mesh['x'=4,'zh'=4,'co'=2,'y'=4,'zq'=4,'zb'=2] {'zh'}, dimensions={0} | all-to-all | bytes 131072 | tf_op jit(solution)/shard_map/all_to_all | solution.py:249
  79.3 2.5 %shard_map.85 = bf16[2,4,4,128,256]{4,3,2,1,0:T(8,128)(2,1)S(1)} custom-call(f32[128,256]{1,0:T(8,128)S(1)} %get-tuple-element.14.gate_ref, bf16[256,128]{1,0:T(8,128)(2,1)S(1)} %get-tuple-element.18.gated_ref, bf16[16,128,256]{2,1,0:T(8,128)(2,1)S(1)} %get-tuple-element.19.lr_ref, f32[4,16,256]{2,1,0:T(8,128)S(1)} %all_to_all.21.far_ref, ...), custom_call_target="tpu_custom_call" | custom-call | tf_op jit(solution)/shard_map/pallas_call | solution.py:194
  81.9 29.6 %all_to_all.22 = bf16[8,4,128,256]{3,2,1,0:T(8,128)(2,1)S(1)} all-to-all(bf16[8,4,128,256]{3,2,1,0:T(8,128)(2,1)S(1)} %bitcast.4), channel_id=1, replica_groups=mesh['x'=4,'zh'=4,'co'=2,'y'=4,'zq'=4,'zb'=2] {'zb','y'}, dimensions={0} | all-to-all | bytes 4194304 | tf_op jit(solution)/shard_map/all_to_all | solution.py:263
  111.5 0.3 reduce_sum.12
  111.8 19.0 %all_to_all.23.far_ref = bf16[4,128,256]{2,1,0:T(8,128)(2,1)S(1)} all-to-all(bf16[4,128,256]{2,1,0:T(8,128)(2,1)S(1)} %reduce_sum.12), channel_id=1, replica_groups=mesh['x'=4,'zh'=4,'co'=2,'y'=4,'zq'=4,'zb'=2] {'zq'}, dimensions={0} | all-to-all | bytes 524288 | tf_op jit(solution)/shard_map/all_to_all | solution.py:271
  130.8 0.7 shard_map.86
  (1 shorter events, 0.0 us)
Async XLA Ops:
  0.9 7.0 %collective-permute-start = (bf16[256,128]{1,0:T(8,128)(2,1)S(1)}, bf16[256,128]{1,0:T(8,128)(2,1)S(1)}, u32[]{:S(2)}, u32[]{:S(2)}) collective-permute-start(bf16[256,128]{1,0:T(8,128)(2,1)S(1)} %multiply_convert_fusion.kv_ref), channel_id=1, source_target_pairs={{0,32},{32,64},{64,96},{96,128},{128,160},{160,192},{192,224},{224... | collective-permute-start | bytes 196616 | tf_op jit(solution)/shard_map/ppermute | solution.py:214
  2.7 0.8 copy-start
  3.6 0.8 copy-start.1
  4.4 0.7 copy-start.2
  5.1 0.7 copy-start.3
  5.8 0.7 copy-start.4
